TPU v7x, 32 devices: a whole 2x2x4 slice. The times are simulated.
32 devices in a mesh: dev: 32 (over z, y, x, core).
Axes of the slice: x: 2, y: 2, z: 4, core: 2. Of those that a mesh axis runs over, the one named last changes fastest.
Arguments:
- conductivity: float32 [128, 3, 2048], P('dev'), may hold values from 0.05 to 1
- block_ids: int32 [64, 16], P('dev'), may hold values from 0 to 127, as said below
- weights: int32 [64, 8], P('dev'), may hold values from 1 to 7
- source: float32 [64, 3, 8, 16, 128], P('dev'), may hold values from -6 to 6
- cotangent: float32 [64, 3, 8, 16, 128], P('dev'), may hold values from -6 to 6
Outputs:
- fields: float32 [64, 3, 8, 16, 128], P('dev')
- gradient: float32 [128, 3, 2048], P('dev')
Inputs may be any that keep to these rules, and one draw needn't show every extreme that they name: `block_ids`: the 32 entries of the meshes of one device (an aligned block of 2 rows) name blocks of all owners, each owner exactly once, the owner of a block being its id // 4.
All inputs are finite; a program needn't handle non-finite values.
Results may differ from a plain program's by a relative error of at most 0.00002.
Values sent between devices are 32-bit elements; how exact they have to be, the bound alone decides.
No kernel may reach another device: no remote copies, remote signals or barrier semaphores. Data moves between devices by JAX's collectives and lax.ppermute only.
A program may use at most 128 MiB of HBM per device.

v0:
```python
import jax
import jax.numpy as jnp
from jax import lax
from jax.sharding import PartitionSpec as P

MX = 8
MY = 16
MZ = 128
STEPS = 10


time_step = 0.5


def difference(values, direction, forward):
    length = values.shape[direction]
    zero_plane = jnp.zeros_like(lax.slice_in_dim(values, 0, 1, axis=direction))
    if forward:
        later = jnp.concatenate(
            [lax.slice_in_dim(values, 1, length, axis=direction), zero_plane], axis=direction
        )
        return later - values
    earlier = jnp.concatenate(
        [zero_plane, lax.slice_in_dim(values, 0, length - 1, axis=direction)], axis=direction
    )
    return values - earlier


def curl_of(vector, forward):
    first = difference(vector[2], 1, forward) - difference(vector[1], 2, forward)
    second = difference(vector[0], 2, forward) - difference(vector[2], 0, forward)
    third = difference(vector[1], 0, forward) - difference(vector[0], 1, forward)
    return jnp.stack([first, second, third])


def evolve(damping, initial):

    def leapfrog(state_pair, unused_item):
        electric, magnetic = state_pair
        magnetic = magnetic - time_step * curl_of(electric, True)
        electric = electric + time_step * (curl_of(magnetic, False) - damping * electric)
        return ((electric, magnetic), None)

    final_pair, unused_out = lax.scan(
        leapfrog, (initial, jnp.zeros_like(initial)), None, length=STEPS
    )
    return final_pair[0]


def mesh_field(picked, mesh_weights, initial):
    fraction = mesh_weights.astype(jnp.float32) / 8.0
    near_part = picked[:MX]
    far_part = picked[MX:]
    damping = fraction[:, None, None] * near_part + (1.0 - fraction)[:, None, None] * far_part
    damping = jnp.swapaxes(damping, 0, 1).reshape(3, MX, MY, MZ)
    return evolve(damping, initial)


def local(conductivity, block_ids, weights, source, cotangent):
    blocks_here = conductivity.shape[0]
    block_cells = conductivity.shape[2]
    device_count = lax.axis_size("dev")
    mesh_count = block_ids.shape[0]
    layer_entries = block_ids.shape[1]
    entry_count = mesh_count * layer_entries
    flat_ids = block_ids.reshape(entry_count)
    owner_index = flat_ids // blocks_here
    local_index = flat_ids % blocks_here
    requested = jnp.full((device_count,), -1, jnp.int32).at[owner_index].set(local_index)
    requested = requested.reshape(device_count, 1)
    incoming = lax.all_to_all(requested, "dev", split_axis=0, concat_axis=0, tiled=True)
    wanted = jnp.clip(incoming.reshape(device_count), 0, blocks_here - 1)
    outgoing = jnp.take(conductivity.reshape(blocks_here, 3 * block_cells), wanted, axis=0)
    arrived = lax.all_to_all(outgoing, "dev", split_axis=0, concat_axis=0, tiled=True)
    picked = jnp.take(arrived, owner_index, axis=0)
    picked = picked.reshape(mesh_count, layer_entries, 3, block_cells)

    def single_mesh(mesh_items):
        mesh_blocks, mesh_weights, mesh_source, mesh_cotangent = mesh_items
        electric, pullback = jax.vjp(
            lambda blocks_in: mesh_field(blocks_in, mesh_weights, mesh_source), mesh_blocks
        )
        (mesh_grads,) = pullback(mesh_cotangent)
        return (electric, mesh_grads)

    fields, grads = lax.map(single_mesh, (picked, weights, source, cotangent))
    outgoing_grads = (
        jnp.zeros((device_count, 3 * block_cells), jnp.float32)
        .at[owner_index]
        .add(grads.reshape(entry_count, 3 * block_cells))
    )
    back_grads, back_ids = (
        lax.all_to_all(outgoing_grads, "dev", split_axis=0, concat_axis=0, tiled=True),
        lax.all_to_all(requested, "dev", split_axis=0, concat_axis=0, tiled=True),
    )
    back_flat = back_ids.reshape(device_count)
    target_rows = jnp.where(back_flat < 0, blocks_here, back_flat)
    gradient = (
        jnp.zeros((blocks_here, 3 * block_cells), jnp.float32)
        .at[target_rows]
        .add(back_grads, mode="drop")
    )
    return (fields, gradient.reshape(blocks_here, 3, block_cells))


def solution(mesh):
    placed = (
        P("dev", None, None),
        P("dev", None),
        P("dev", None),
        P("dev", None, None, None, None),
        P("dev", None, None, None, None),
    )
    return jax.shard_map(
        local,
        mesh=mesh,
        in_specs=placed,
        out_specs=(P("dev", None, None, None, None), P("dev", None, None)),
        check_vma=False,
    )
```

profile of v0, /device:TPU:0, one launch (start us, length us, event | category | flops | bytes accessed | tf_op | source)
XLA Modules:
  0.0 120.5 jit_solution(74136312178195899)
XLA Ops:
  0.6 0.8 reshape.265
  1.4 0.8 reshape.266
  2.2 0.7 scatter_custom_fusion
  3.0 14.3 %all_to_all.34 = s32[32,1,1]{2,1,0:T(1,128)S(1)} all-to-all(s32[32,1,1]{2,1,0:T(1,128)S(1)} %copy.15), channel_id=1, replica_groups=mesh['dev'=32] {'dev'}, dimensions={0} | all-to-all | bytes 256 | tf_op jit(solution)/shard_map/all_to_all | solution.py:71
  17.3 1.2 %clamp_reduce_fusion = (s32[32]{0:T(128)S(1)}, s32[32]{0:T(128)S(1)}) fusion(s32[32,1,1]{2,1,0:T(1,128)S(1)} %all_to_all.34), kind=kLoop, calls=%fused_computation.91 | loop fusion | flops 32 | bytes 384 | tf_op jit(solution)/shard_map/jit(clip)/min | solution.py:72
  18.6 0.8 gather_fusion
  19.5 1.7 %copy.16 = f32[32,1,6144]{2,1,0:T(1,128)} copy(f32[32,1,6144]{2,0,1:T(8,128)S(1)} %bitcast_select_fusion) | data formatting | bytes 1572864 | tf_op jit(solution)/shard_map/jit(_take)/select_n | solution.py:73
  21.2 2.6 %all-to-all-start.1 = ((f32[32,1,6144]{2,1,0:T(1,128)}), f32[32,1,6144]{2,1,0:T(1,128)S(1)}, u32[]{:S(2)}, u32[]{:S(2)}) async-start(f32[32,1,6144]{2,1,0:T(1,128)} %copy.16), calls=%async_computation.1 | async-start | bytes 1572864 | tf_op jit(solution)/shard_map/all_to_all | solution.py:74
  23.9 20.5 %all-to-all-done.1 = f32[32,1,6144]{2,1,0:T(1,128)S(1)} async-done(((f32[32,1,6144]{2,1,0:T(1,128)}), f32[32,1,6144]{2,1,0:T(1,128)S(1)}, u32[]{:S(2)}, u32[]{:S(2)}) %all-to-all-start.1) | async-done | bytes 786464 | tf_op jit(solution)/shard_map/all_to_all | solution.py:74
  44.4 0.2 copy.30
  44.7 0.8 gather_fusion.1
  45.5 0.6 gather.15
  46.1 0.3 broadcast_select_fusion
  46.4 1.4 %copy.17 = f32[2,16,3,2048]{3,1,2,0:T(8,128)} copy(f32[2,16,3,2048]{3,2,1,0:T(4,128)S(1)} %broadcast_select_fusion) | data formatting | bytes 1572864 | tf_op jit(solution)/shard_map/while | solution.py:86
  47.8 39.7 %while.83 = (s32[]{:T(128)}, f32[2,3,8,16,128]{4,3,2,1,0:T(8,128)}, f32[2,16,3,2048]{3,1,2,0:T(8,128)}, f32[2,3,8,16,128]{4,3,2,1,0:T(8,128)}, s32[2,8]{1,0:T(2,...) while((s32[]{:T(128)}, f32[2,3,8,16,128]{4,3,2,1,0:T(8,128)}, ...), condition=%wide.region_6.7_spmd, body=%wide.region_1.6_spmd.sunk | while | flops 2637858 | bytes 16115436 | solution.py:86
  47.8 1.1 fusion.41
  48.9 1.1 dynamic-slice_bitcast_fusion.5
  50.0 7.0 %while.84 = (s32[]{:T(128)}, f32[3,8,16,128]{3,2,1,0:T(8,128)S(1)}, f32[3,8,16,128]{3,2,1,0:T(8,128)S(1)}, f32[10,3,8,16,128]{4,3,2,1,0:T(8,128)S(1)}, f32[3,8,16,128]{3,2,1,0:T(8,128)S(1)}, /*index=5*/s32[]{:T(128)}, s32[]{:T(128)}) while((s32[]{:T(128)}, f32[3,8,16,128]{3,2,1,0:T(8,128)S(1)}, f32[3,8,16,128]{3,2,1,0:T(8,128)S(1)}, ...), condition=%wide.region_3.3_spmd.clone, body=%wide.region_2.2_spmd.clone.sunk | while | flops 835587 | bytes 5042267 | solution.py:44
  57.0 9.0 %while.85 = (s32[]{:T(128)}, f32[3,8,16,128]{3,2,1,0:T(8,128)S(1)}, f32[3,8,16,128]{3,2,1,0:T(8,128)S(1)}, f32[3,8,16,128]{3,2,1,0:T(8,128)S(1)}, f32[10,3,8,16,...) while((s32[]{:T(128)}, f32[3,8,16,128]{3,2,1,0:T(8,128)S(1)}, ...), condition=%wide.region_5.5_spmd.clone, body=%wide.region_4.4_spmd.clone.sunk | while | flops 1458180 | bytes 7139448 | solution.py:44
  57.7 0.2 pad_add_fusion.2
  58.6 0.2 pad_add_fusion.2
  59.5 0.2 pad_add_fusion.2
  60.4 0.2 pad_add_fusion.2
  61.3 0.2 pad_add_fusion.2
  62.2 0.2 pad_add_fusion.2
  63.1 0.2 pad_add_fusion.2
  64.0 0.2 pad_add_fusion.2
  64.9 0.2 pad_add_fusion.2
  65.8 0.2 pad_add_fusion.2
  66.1 0.8 bitcast_dynamic-update-slice_fusion.7
  66.9 0.7 bitcast_dynamic-update-slice_fusion.6
  67.6 1.1 fusion.41
  68.8 1.1 dynamic-slice_bitcast_fusion.5
  69.8 7.0 %while.84 = (s32[]{:T(128)}, f32[3,8,16,128]{3,2,1,0:T(8,128)S(1)}, f32[3,8,16,128]{3,2,1,0:T(8,128)S(1)}, f32[10,3,8,16,128]{4,3,2,1,0:T(8,128)S(1)}, f32[3,8,16,128]{3,2,1,0:T(8,128)S(1)}, /*index=5*/s32[]{:T(128)}, s32[]{:T(128)}) while((s32[]{:T(128)}, f32[3,8,16,128]{3,2,1,0:T(8,128)S(1)}, f32[3,8,16,128]{3,2,1,0:T(8,128)S(1)}, ...), condition=%wide.region_3.3_spmd.clone, body=%wide.region_2.2_spmd.clone.sunk | while | flops 835587 | bytes 5042267 | solution.py:44
  76.9 9.0 %while.85 = (s32[]{:T(128)}, f32[3,8,16,128]{3,2,1,0:T(8,128)S(1)}, f32[3,8,16,128]{3,2,1,0:T(8,128)S(1)}, f32[3,8,16,128]{3,2,1,0:T(8,128)S(1)}, f32[10,3,8,16,...) while((s32[]{:T(128)}, f32[3,8,16,128]{3,2,1,0:T(8,128)S(1)}, ...), condition=%wide.region_5.5_spmd.clone, body=%wide.region_4.4_spmd.clone.sunk | while | flops 1458180 | bytes 7139448 | solution.py:44
  77.6 0.2 pad_add_fusion.2
  78.5 0.2 pad_add_fusion.2
  79.4 0.2 pad_add_fusion.2
  80.3 0.2 pad_add_fusion.2
  82.1 0.2 pad_add_fusion.2
  86.0 0.8 bitcast_dynamic-update-slice_fusion.7
  86.8 0.7 bitcast_dynamic-update-slice_fusion.6
  87.5 1.7 %copy.18 = f32[2,16,3,2048]{3,2,1,0:T(4,128)S(1)} copy(f32[2,16,3,2048]{3,1,2,0:T(8,128)} %get-tuple-element.317) | data formatting | bytes 1572864 | tf_op jit(solution)/shard_map/while | solution.py:86
  89.1 0.5 copy.22
  89.6 1.7 %scatter_custom_fusion.1 = f32[32,6144]{1,0:T(8,128)S(1)} fusion(s32[32]{0:T(128)S(1)} %fusion.29, f32[32,6144]{1,0:T(8,128)S(1)} %bitcast.303, f32[]{:T(128)} %constant.182.clone.1), kind=kCustom, calls=%fused_computation.88 | custom fusion | flops 196608 | bytes 786436 | tf_op jit(solution)/shard_map/scatter-add | solution.py:90
  91.3 0.5 all_to_all.28
  91.8 23.9 %all_to_all.35 = f32[32,1,6144]{2,1,0:T(1,128)S(1)} all-to-all(f32[32,1,6144]{2,1,0:T(1,128)S(1)} %all_to_all.28), channel_id=1, replica_groups=mesh['dev'=32] {'dev'}, dimensions={0} | all-to-all | bytes 1572864 | tf_op jit(solution)/shard_map/all_to_all | solution.py:93
  115.8 4.7 %scatter_custom_fusion.2 = f32[4,6144]{1,0:T(4,128)} fusion(s32[32]{0:T(128)S(1)} %get-tuple-element.462, f32[32,1,6144]{2,1,0:T(1,128)S(1)} %all_to_all.35, f32[]{:T(128)} %constant.182.clone.1), kind=kCustom, calls=%fused_computation.82 | custom fusion | flops 196608 | bytes 884740 | tf_op jit(solution)/shard_map/scatter-add | solution.py:101
  (658 shorter events, 25.7 us)
Async XLA Ops:
  0.6 17.9 %copy-start = (f32[4,3,2048]{2,0,1:T(4,128)S(1)}, f32[4,3,2048]{2,0,1:T(4,128)}, u32[]{:S(2)}) copy-start(f32[4,3,2048]{2,0,1:T(4,128)} %param.11) | copy-start | bytes 294916
  19.5 4.4 %copy-start.2 = (s32[2,16]{1,0:T(2,128)S(1)}, s32[2,16]{1,0:T(2,128)}, u32[]{:S(2)}) copy-start(s32[2,16]{1,0:T(2,128)} %param.12) | copy-start | bytes 388
  21.2 23.2 %all-to-all-start.1 = ((f32[32,1,6144]{2,1,0:T(1,128)}), f32[32,1,6144]{2,1,0:T(1,128)S(1)}, u32[]{:S(2)}, u32[]{:S(2)}) async-start(f32[32,1,6144]{2,1,0:T(1,128)} %copy.16), calls=%async_computation.1 | async-start | bytes 1572864 | tf_op jit(solution)/shard_map/all_to_all | solution.py:74
  46.1 1.7 %copy-start.1 = (s32[2,8]{1,0:T(2,128)S(1)}, s32[2,8]{1,0:T(2,128)}, u32[]{:S(2)}) copy-start(s32[2,8]{1,0:T(2,128)} %param.13) | copy-start | bytes 196
where the time goes:
time: 121 us; the launch traced here: 120 us
  blocking collectives  38.2 us (32%)
  other arithmetic  30.2 us (25%)
  local copies, waits for them, and re-layouts  23.5 us (19%)
  waiting for transfers between devices  20.5 us (17%)
  loops' own time  4.58 us (4%)
  starting transfers between devices  2.62 us (2%)
    all_to_all x1, blocking collectives, local(): lax.all_to_all(outgoing_grads, 'dev', split_axis=0, concat_axis=0, tiled=...  23.9 us
    all_to_all x1, waiting for transfers between devices, local(): lax.all_to_all(outgoing, 'dev', split_axis=0, concat_axis=0, tiled=True)  20.5 us
    all_to_all x1, blocking collectives, local(): lax.all_to_all(requested, 'dev', split_axis=0, concat_axis=0, tiled=True)  14.3 us
    scatter-add x1, other arithmetic, local(): gradient = jnp.zeros((blocks_here, 3 * block_cells), jnp.float32).at[targ...  4.7 us
    another operation x4, loops' own time, evolve(): lax.scan(leapfrog, (initial, jnp.zeros_like(initial)), None, length=STEPS)  4.44 us
    slice x100, local copies, waits for them, and re-layouts, difference(): lax.slice_in_dim(values, 1, length, axis=direction)  3.88 us
    split x120, local copies, waits for them, and re-layouts, difference(): jnp.concatenate([zero_plane, lax.slice_in_dim(values, 0, length - 1, axis...  3.65 us
    another operation x40, other arithmetic, curl_of(): return jnp.stack([first, second, third])  3.43 us
  transfers between devices with their start and end apart: 1, of which 1 were waited for; matrix products, arithmetic and copies ran while one was open for 0% of the time, Pallas kernels for 0%

commit v1 on v0

v1 whole, which is shorter than its diff:
```python
import functools

import jax
import jax.numpy as jnp
from jax import lax
from jax.experimental import pallas as pl
from jax.experimental.pallas import tpu as pltpu
from jax.sharding import PartitionSpec as P

STEPS = 10
ANY = pl.BlockSpec(memory_space=pl.ANY)
VMEM = pl.BlockSpec(memory_space=pltpu.VMEM)
SMEM = pl.BlockSpec(memory_space=pltpu.SMEM)


def request_kernel(count, blocks_here, ids_ref, out_ref):
    entries = ids_ref.shape[1]

    def one(entry, carry):
        block = ids_ref[entry // entries, entry % entries]
        out_ref[block // blocks_here, 0, 0] = block % blocks_here
        return carry

    lax.fori_loop(0, count, one, 0, unroll=8)


def gather_kernel(count, blocks_here, wanted_ref, rows_ref, out_ref):
    rows = out_ref.shape[1]
    for peer in range(count):
        row = wanted_ref[peer, 0, 0]
        out_ref[peer] = rows_ref[pl.ds(row, rows, stride=blocks_here), :]


def scatter_kernel(count, blocks_here, wanted_ref, in_ref, out_ref, total):
    rows = in_ref.shape[1]
    total[...] = jnp.zeros_like(total)
    for peer in range(count):
        row = wanted_ref[peer, 0, 0]
        total[row] = total[row] + in_ref[peer]
    for block in range(blocks_here):
        out_ref[pl.ds(block, rows, stride=blocks_here), :] = total[block]


def mesh_kernel(
    blocks_here,
    ids_ref,
    weights_ref,
    arrived_ref,
    source_ref,
    cotangent_ref,
    fields_ref,
    grads_ref,
    history,
    magnetic,
    keep,
    in_sem,
    out_sem,
):
    meshes = source_ref.shape[0]
    layers, height, width = source_ref.shape[2:]
    slots = history.shape[0]
    parts = 3

    def incoming(mesh, slot):
        return [
            pltpu.make_async_copy(ref.at[mesh], history.at[slot, run, 0], in_sem.at[slot, run])
            for run, ref in enumerate((source_ref, cotangent_ref))
        ]

    def outgoing(mesh, slot):
        return pltpu.make_async_copy(
            history.at[slot, 0, STEPS], fields_ref.at[mesh], out_sem.at[slot]
        )

    for mesh in range(slots):
        for copy in incoming(mesh, mesh):
            copy.start()

    lane = lax.broadcasted_iota(jnp.int32, (height, width), 1)
    line = lax.broadcasted_iota(jnp.int32, (height, width), 0)
    last_lane, first_lane = lane == width - 1, lane == 0
    last_line, first_line = line == height - 1, line == 0

    def plus_z(v):
        return jnp.where(last_lane, 0.0, pltpu.roll(v, width - 1, 1)) - v

    def plus_y(v):
        return jnp.where(last_line, 0.0, pltpu.roll(v, height - 1, 0)) - v

    def minus_z(v):
        return v - jnp.where(first_lane, 0.0, pltpu.roll(v, 1, 1))

    def minus_y(v):
        return v - jnp.where(first_line, 0.0, pltpu.roll(v, 1, 0))

    def sweep(slot, step, runs):
        for run in runs:
            now = [history[slot, run, step, c, 0] for c in range(parts)]
            below = None
            for layer in range(layers):
                ex, ey, ez = now
                if layer + 1 < layers:
                    above = [history[slot, run, step, c, layer + 1] for c in range(parts)]
                    dx_y, dx_z = above[1] - ey, above[2] - ez
                else:
                    above = None
                    dx_y, dx_z = -ey, -ez
                gx = magnetic[run, 0, layer] - 0.25 * (plus_y(ez) - plus_z(ey))
                gy = magnetic[run, 1, layer] - 0.25 * (plus_z(ex) - dx_z)
                gz = magnetic[run, 2, layer] - 0.25 * (dx_y - plus_y(ex))
                magnetic[run, 0, layer] = gx
                magnetic[run, 1, layer] = gy
                magnetic[run, 2, layer] = gz
                if below is None:
                    bx_y, bx_z = gy, gz
                else:
                    bx_y, bx_z = gy - below[0], gz - below[1]
                below = (gy, gz)
                history[slot, run, step + 1, 0, layer] = keep[0, layer] * ex + (
                    minus_y(gz) - minus_z(gy)
                )
                history[slot, run, step + 1, 1, layer] = keep[1, layer] * ey + (
                    minus_z(gx) - bx_z
                )
                history[slot, run, step + 1, 2, layer] = keep[2, layer] * ez + (
                    bx_y - minus_y(gx)
                )
                now = above

    def one_mesh(mesh, carry):
        slot = lax.rem(mesh, slots)
        for layer in range(layers):
            fraction = weights_ref[mesh, layer].astype(jnp.float32) * 0.125
            near = ids_ref[mesh, layer] // blocks_here
            far = ids_ref[mesh, layer + layers] // blocks_here
            for c in range(parts):
                rows = pl.ds(c * height, height)
                keep[c, layer] = 1.0 - 0.5 * (
                    fraction * arrived_ref[near, rows] + (1.0 - fraction) * arrived_ref[far, rows]
                )
        magnetic[...] = jnp.zeros_like(magnetic)
        for copy in incoming(mesh, slot):
            copy.wait()

        @pl.when(mesh >= slots)
        def _():
            outgoing(mesh - slots, slot).wait()

        def step_of(step, inner):
            sweep(slot, step, (0, 1))
            return inner

        lax.fori_loop(0, STEPS - 1, step_of, 0)
        sweep(slot, STEPS - 1, (0,))
        outgoing(mesh, slot).start()
        for layer in range(layers):
            fraction = weights_ref[mesh, layer].astype(jnp.float32) * 0.125
            near = ids_ref[mesh, layer] // blocks_here
            far = ids_ref[mesh, layer + layers] // blocks_here
            for c in range(parts):
                rows = pl.ds(c * height, height)
                total = None
                for step in range(STEPS):
                    term = history[slot, 0, step, c, layer] * history[slot, 1, STEPS - 1 - step, c, layer]
                    total = term if total is None else total + term
                total = -0.5 * total
                grads_ref[near, rows] = fraction * total
                grads_ref[far, rows] = (1.0 - fraction) * total

        @pl.when(mesh + slots < meshes)
        def _():
            for copy in incoming(mesh + slots, slot):
                copy.start()

        return carry

    lax.fori_loop(0, meshes, one_mesh, 0)
    for mesh in range(meshes - slots, meshes):
        outgoing(mesh, mesh % slots).wait()


def local(conductivity, block_ids, weights, source, cotangent):
    blocks_here, parts, cells = conductivity.shape
    meshes, _, layers, height, width = source.shape
    count = lax.axis_size("dev")
    rows = parts * cells // width
    f32 = jnp.float32
    requested = pl.pallas_call(
        functools.partial(request_kernel, block_ids.size, blocks_here),
        out_shape=jax.ShapeDtypeStruct((count, 1, 1), jnp.int32),
        in_specs=[SMEM],
        out_specs=SMEM,
        name="requests",
    )(block_ids)
    wanted = lax.all_to_all(requested, "dev", split_axis=0, concat_axis=0, tiled=True)
    own_rows = (
        conductivity.reshape(blocks_here, rows, width).transpose(1, 0, 2).reshape(-1, width)
    )
    outgoing = pl.pallas_call(
        functools.partial(gather_kernel, count, blocks_here),
        out_shape=jax.ShapeDtypeStruct((count, rows, width), f32),
        in_specs=[SMEM, VMEM],
        out_specs=VMEM,
        compiler_params=pltpu.CompilerParams(vmem_limit_bytes=16 << 20),
        name="collect",
    )(wanted, own_rows)
    arrived = lax.all_to_all(outgoing, "dev", split_axis=0, concat_axis=0, tiled=True)
    slots = min(meshes, 2)
    fields, grads = pl.pallas_call(
        functools.partial(mesh_kernel, blocks_here),
        out_shape=(
            jax.ShapeDtypeStruct(source.shape, f32),
            jax.ShapeDtypeStruct((count, rows, width), f32),
        ),
        in_specs=[SMEM, SMEM, VMEM, ANY, ANY],
        out_specs=(ANY, VMEM),
        scratch_shapes=[
            pltpu.VMEM((slots, 2, STEPS + 1, parts, layers, height, width), f32),
            pltpu.VMEM((2, parts, layers, height, width), f32),
            pltpu.VMEM((parts, layers, height, width), f32),
            pltpu.SemaphoreType.DMA((slots, 2)),
            pltpu.SemaphoreType.DMA((slots,)),
        ],
        compiler_params=pltpu.CompilerParams(vmem_limit_bytes=32 << 20),
        name="leapfrog",
    )(block_ids, weights, arrived, source, cotangent)
    returned = lax.all_to_all(grads, "dev", split_axis=0, concat_axis=0, tiled=True)
    gradient = pl.pallas_call(
        functools.partial(scatter_kernel, count, blocks_here),
        out_shape=jax.ShapeDtypeStruct((rows * blocks_here, width), f32),
        in_specs=[SMEM, VMEM],
        out_specs=VMEM,
        scratch_shapes=[pltpu.VMEM((blocks_here, rows, width), f32)],
        compiler_params=pltpu.CompilerParams(vmem_limit_bytes=16 << 20),
        name="deposit",
    )(wanted, returned)
    gradient = gradient.reshape(rows, blocks_here, width).transpose(1, 0, 2)
    return fields, gradient.reshape(conductivity.shape)


def solution(mesh):
    placed = (
        P("dev", None, None),
        P("dev", None),
        P("dev", None),
        P("dev", None, None, None, None),
        P("dev", None, None, None, None),
    )
    return jax.shard_map(
        local,
        mesh=mesh,
        in_specs=placed,
        out_specs=(P("dev", None, None, None, None), P("dev", None, None)),
        check_vma=False,
    )
```

time: 121 us -> 75.2 us (0.62)
  other arithmetic: 30.2 us -> 0 us
  blocking collectives: 38.2 us -> 60.8 us
  local copies, waits for them, and re-layouts: 23.5 us -> 0.92 us
  waiting for transfers between devices: 20.5 us -> 0 us
  Pallas kernels: 0 us -> 12.5 us
  loops' own time: 4.58 us -> 0 us
  starting transfers between devices: 2.62 us -> 0 us
    all_to_all x1 -> x2, blocking collectives: 23.9 us -> 46.4 us  [the longest x1 23.9 us: local(): lax.all_to_all(grads, 'dev', split_axis=0, concat_axis=0, tiled=True)]
    all_to_all x1 -> x0, waiting for transfers between devices: 20.5 us -> none  [local(): lax.all_to_all(outgoing, 'dev', split_axis=0, concat_axis=0, tiled=True)]
    pallas_call x0 -> x4, Pallas kernels: none -> 12.5 us  [the longest x1 8.1 us: local(): pl.pallas_call(functools.partial(mesh_kernel, blocks_here), out_shape=(ja...]
    scatter-add x2 -> x0, other arithmetic: 6.39 us -> none  [the longest x1 4.7 us: local(): gradient = jnp.zeros((blocks_here, 3 * block_cells), jnp.float32).at[targ...]
    broadcast_in_dim x82 -> x0, other arithmetic: 4.63 us -> none  [the longest x40 2.52 us: curl_of(): vector[0]]
    another operation x5 -> x0, loops' own time: 4.58 us -> none  [the longest x4 4.44 us: evolve(): lax.scan(leapfrog, (initial, jnp.zeros_like(initial)), None, length=STEPS)]
    slice x120 -> x0, local copies, waits for them, and re-layouts: 4.08 us -> none  [the longest x100 3.88 us: difference(): lax.slice_in_dim(values, 1, length, axis=direction)]
    split x160 -> x0, local copies, waits for them, and re-layouts: 3.88 us -> none  [the longest x120 3.65 us: difference(): jnp.concatenate([zero_plane, lax.slice_in_dim(values, 0, length - 1, axis...]
  transfers between devices with their start and end apart: 1 -> 0, of which waited for: 1 -> 0; matrix products, arithmetic and copies ran while one was open for 0% -> 0% of each run, Pallas kernels for 0% -> 0%
where the time goes in v1:
time: 75.2 us; the launch traced here: 74.9 us
  blocking collectives  60.8 us (81%)
  Pallas kernels  12.5 us (17%)
  local copies, waits for them, and re-layouts  0.92 us (1%)
    all_to_all x1, blocking collectives, local(): lax.all_to_all(grads, 'dev', split_axis=0, concat_axis=0, tiled=True)  23.9 us
    all_to_all x1, blocking collectives, local(): lax.all_to_all(outgoing, 'dev', split_axis=0, concat_axis=0, tiled=True)  22.4 us
    all_to_all x1, blocking collectives, local(): lax.all_to_all(requested, 'dev', split_axis=0, concat_axis=0, tiled=True)  14.4 us
    pallas_call x1, Pallas kernels, local(): pl.pallas_call(functools.partial(mesh_kernel, blocks_here), out_shape=(ja...  8.1 us
    pallas_call x1, Pallas kernels, local(): pl.pallas_call(functools.partial(request_kernel, block_ids.size, blocks_h...  1.89 us
    pallas_call x1, Pallas kernels, local(): pl.pallas_call(functools.partial(scatter_kernel, count, blocks_here), out...  1.61 us

profile of v1, /device:TPU:0, one launch (start us, length us, event | category | flops | bytes accessed | tf_op | source)
XLA Modules:
  0.0 74.9 jit_solution(12017226696706855341)
XLA Ops:
  0.6 1.9 %requests.1 = s32[32,1,1]{2,1,0:T(1,128)} custom-call(s32[2,16]{1,0:T(2,128)} %ids_ref.3), custom_call_target="tpu_custom_call" | custom-call | tf_op jit(solution)/shard_map/requests/pallas_call | solution.py:188
  2.5 14.4 %all_to_all.15.wanted_ref = s32[32,1,1]{2,1,0:T(1,128)S(1)} all-to-all(s32[32,1,1]{2,1,0:T(1,128)} %requests.1), channel_id=1, replica_groups=mesh['dev'=32] {'dev'}, dimensions={0} | all-to-all | bytes 256 | tf_op jit(solution)/shard_map/all_to_all | solution.py:195
  17.0 0.0 copy-start.2
  17.0 0.9 %copy-done.2 = f32[4,3,2048]{2,0,1:T(4,128)S(1)} copy-done((f32[4,3,2048]{2,0,1:T(4,128)S(1)}, f32[4,3,2048]{2,0,1:T(4,128)}, u32[]{:S(2)}) %copy-start.2) | copy-done | bytes 98328
  17.9 0.9 %collect.1 = f32[32,48,128]{2,1,0:T(8,128)S(1)} custom-call(s32[32,1,1]{2,1,0:T(1,128)S(1)} %all_to_all.15.wanted_ref, f32[192,128]{1,0:T(8,128)S(1)} %bitcast.10), custom_call_target="tpu_custom_call" | custom-call | tf_op jit(solution)/shard_map/collect/pallas_call | solution.py:199
  18.8 0.0 copy-start
  18.8 0.0 copy-start.1
  18.8 0.0 copy-start.3
  18.8 0.0 copy-start.4
  18.8 22.4 %all_to_all.16.arrived_ref = f32[32,48,128]{2,1,0:T(8,128)S(1)} all-to-all(f32[32,48,128]{2,1,0:T(8,128)S(1)} %collect.1), channel_id=1, replica_groups=mesh['dev'=32] {'dev'}, dimensions={0} | all-to-all | bytes 1572864 | tf_op jit(solution)/shard_map/all_to_all | solution.py:207
  41.3 0.0 copy-done
  41.3 0.0 copy-done.1
  41.3 0.0 copy-done.3
  41.3 0.0 copy-done.4
  41.3 8.1 %leapfrog.1 = (f32[2,3,8,16,128]{4,3,2,1,0:T(8,128)}, f32[32,48,128]{2,1,0:T(8,128)S(1)}) custom-call(s32[2,16]{1,0:T(2,128)S(1)} %copy-done.3, s32[2,8]{1,0:T(2,128)S(1)} %copy-done.4, f32[32,48,128]{2,1,0:T(8,128)S(1)} %all_to_all.16.arrived_ref, f32[2,3,8,16,128]{4,3,2,1,0:T(8,128)S(1)} %copy-done, f32[2,3,8,16,128]{4,3,2,1,0:T(8,128)S(1)} %copy-done.1), custom_call_target="tpu_custom_call" | custom-call | tf_op jit(solution)/shard_map/leapfrog/pallas_call | solution.py:209
  49.4 23.9 %all_to_all.17.in_ref = f32[32,48,128]{2,1,0:T(8,128)S(1)} all-to-all(f32[32,48,128]{2,1,0:T(8,128)S(1)} %get-tuple-element.5), channel_id=1, replica_groups=mesh['dev'=32] {'dev'}, dimensions={0} | all-to-all | bytes 1572864 | tf_op jit(solution)/shard_map/all_to_all | solution.py:227
  73.3 1.6 %deposit.1 = f32[192,128]{1,0:T(8,128)} custom-call(s32[32,1,1]{2,1,0:T(1,128)S(1)} %all_to_all.15.wanted_ref, f32[32,48,128]{2,1,0:T(8,128)S(1)} %all_to_all.17.in_ref), custom_call_target="tpu_custom_call" | custom-call | tf_op jit(solution)/shard_map/deposit/pallas_call | solution.py:228
Async XLA Ops:
  17.0 0.9 %copy-start.2 = (f32[4,3,2048]{2,0,1:T(4,128)S(1)}, f32[4,3,2048]{2,0,1:T(4,128)}, u32[]{:S(2)}) copy-start(f32[4,3,2048]{2,0,1:T(4,128)} %param.5) | copy-start | bytes 294916
  18.8 22.5 %copy-start = (f32[2,3,8,16,128]{4,3,2,1,0:T(8,128)S(1)}, f32[2,3,8,16,128]{4,3,2,1,0:T(8,128)}, u32[]{:S(2)}) copy-start(f32[2,3,8,16,128]{4,3,2,1,0:T(8,128)} %source_ref.1) | copy-start | bytes 1179652
  18.8 22.5 %copy-start.1 = (f32[2,3,8,16,128]{4,3,2,1,0:T(8,128)S(1)}, f32[2,3,8,16,128]{4,3,2,1,0:T(8,128)}, u32[]{:S(2)}) copy-start(f32[2,3,8,16,128]{4,3,2,1,0:T(8,128)} %cotangent_ref.1) | copy-start | bytes 1179652
  18.8 22.5 %copy-start.3 = (s32[2,16]{1,0:T(2,128)S(1)}, s32[2,16]{1,0:T(2,128)}, u32[]{:S(2)}) copy-start(s32[2,16]{1,0:T(2,128)} %ids_ref.3) | copy-start | bytes 388
  18.8 22.5 %copy-start.4 = (s32[2,8]{1,0:T(2,128)S(1)}, s32[2,8]{1,0:T(2,128)}, u32[]{:S(2)}) copy-start(s32[2,8]{1,0:T(2,128)} %weights_ref.1) | copy-start | bytes 196

commit v2 on v1

v2 whole, which is shorter than its diff:
```python
import functools

import jax
import jax.numpy as jnp
from jax import lax
from jax.experimental import pallas as pl
from jax.experimental.pallas import tpu as pltpu
from jax.sharding import PartitionSpec as P


STEPS = 10
PARTS = 3
PLANE = 4
HBM = pl.BlockSpec(memory_space=pltpu.HBM)
VMEM = pl.BlockSpec(memory_space=pltpu.VMEM)
SMEM = pl.BlockSpec(memory_space=pltpu.SMEM)


def limit(mib):
    return pltpu.CompilerParams(vmem_limit_bytes=mib << 20)


def split_block(block, blocks_here):
    if blocks_here & (blocks_here - 1) == 0:
        shift = blocks_here.bit_length() - 1
        owner = lax.shift_right_logical(block, shift)
        return owner, block & (blocks_here - 1)
    owner = lax.div(block, blocks_here)
    return owner, block - owner * blocks_here


def offset(column, side, core):
    return (column * PLANE + side) * 2 + core


def fill_rows(ids_ref, blocks_here, table, *lead):
    meshes, entries = ids_ref.shape

    def one_mesh(mesh, carry):
        for entry in range(entries):
            owner, row = split_block(ids_ref[mesh, entry], blocks_here)
            table[(*lead, owner)] = row
        return carry

    lax.fori_loop(0, meshes, one_mesh, 0)


def copy_rows(table_ref, group, unit_refs, out_refs, blocks_here):
    rows = out_refs[0].shape[1]
    for place, column in enumerate(group):
        for core in range(2):
            for side in range(1, PLANE):
                row = table_ref[side, 2 * column + core]
                out_refs[side - 1][2 * place + core] = unit_refs[2 * place + core][
                    pl.ds(row, rows, stride=blocks_here), :
                ]


def lookup_kernel(columns, blocks_here, *refs):
    ids_refs, (table_ref, spread) = refs[:PLANE], refs[PLANE:]
    me = lax.axis_index("dev")
    for side in range(PLANE):
        fill_rows(ids_refs[side], blocks_here, spread, side)
    for side in range(PLANE):
        for column in range(columns):
            for core in range(2):
                owner = me ^ offset(column, 0, core)
                table_ref[side, 2 * column + core] = spread[side, owner]


def gather_kernel(group, blocks_here, table_ref, *refs):
    copy_rows(table_ref, group, refs[: 2 * len(group)], refs[2 * len(group) :], blocks_here)


def partner_kernel(group, core, table_ref, own_ref, *refs):
    in_refs, refs = refs[: PLANE - 1], refs[PLANE - 1 :]
    if core == 0:
        partner_ref, out_refs = refs[0], refs[1:]
    else:
        out_refs = refs
    for place, column in enumerate(group):
        out_ref = out_refs[place] if core == 0 else out_refs[0].at[place]
        if core == 0:
            out_ref[...] = partner_ref[place]
        else:
            out_ref[...] = jnp.zeros_like(out_ref)
        for side in range(PLANE):
            row = table_ref[side, 2 * column + core]
            if side == 0:
                value = own_ref[2 * column + core]
            else:
                value = in_refs[side - 1][2 * place + core]
            out_ref[row] = out_ref[row] + value


def final_kernel(*refs):
    in_refs, out_ref = refs[:-1], refs[-1]
    blocks_here, rows = in_refs[0].shape[:2]
    for block in range(blocks_here):
        total = in_refs[0][block]
        for ref in in_refs[1:]:
            total = total + ref[block]
        out_ref[pl.ds(block, rows, stride=blocks_here), :] = total


def mesh_kernel(columns, back_groups, blocks_here, *refs):
    sides = PLANE - 1
    ids_ref, weights_ref, source_ref, cotangent_ref = refs[:4]
    rest = refs[4:]
    unit_refs, rest = rest[: 2 * columns], rest[2 * columns :]
    near_refs, rest = rest[: 2 * sides], rest[2 * sides :]
    side_in = None
    if columns > 1:
        side_in, rest = rest[:sides], rest[sides:]
    fields_ref, own_out = rest[:2]
    rest = rest[2:]
    side_out = rest[: len(back_groups) * sides]
    history, magnetic, keep, picked, sums, entry_of, in_sem, out_sem = rest[
        len(back_groups) * sides :
    ]

    meshes = source_ref.shape[0]
    layers, height, width = source_ref.shape[2:]
    entries = 2 * layers
    slots = history.shape[0]
    rows = PARTS * height
    me = lax.axis_index("dev")

    def incoming(mesh, slot):
        return [
            pltpu.make_async_copy(ref.at[mesh], history.at[slot, run, 0], in_sem.at[slot, run])
            for run, ref in enumerate((source_ref, cotangent_ref))
        ]

    def outgoing(mesh, slot):
        return pltpu.make_async_copy(
            history.at[slot, 0, STEPS], fields_ref.at[mesh], out_sem.at[slot]
        )

    for mesh in range(slots):
        for copy in incoming(mesh, mesh):
            copy.start()

    def note_entries(mesh, carry):
        for entry in range(entries):
            owner, _ = split_block(ids_ref[mesh, entry], blocks_here)
            entry_of[owner] = mesh * entries + entry
        return carry

    lax.fori_loop(0, meshes, note_entries, 0)

    def place_of(column, side, core):
        entry = entry_of[me ^ offset(column, side, core)]
        mesh = lax.div(entry, entries)
        inner = entry - mesh * entries
        far = inner >= layers
        layer = jnp.where(far, inner - layers, inner)
        fraction = weights_ref[mesh, layer].astype(jnp.float32) * 0.125
        return entry, mesh, inner, layer, jnp.where(far, 1.0 - fraction, fraction)

    for column in range(columns):
        for core in range(2):
            for side in range(PLANE):
                entry, mesh, inner, _, share = place_of(column, side, core)
                if side and column:
                    values = side_in[side - 1][2 * (column - 1) + core]
                else:
                    _, row = split_block(ids_ref[mesh, inner], blocks_here)
                    dense = near_refs[2 * (side - 1) + core] if side else unit_refs[2 * column + core]
                    values = dense[pl.ds(row, rows, stride=blocks_here), :]
                picked[entry] = share * values

    lane = lax.broadcasted_iota(jnp.int32, (height, width), 1)
    line = lax.broadcasted_iota(jnp.int32, (height, width), 0)
    last_lane, first_lane = lane == width - 1, lane == 0
    last_line, first_line = line == height - 1, line == 0

    def plus_z(v):
        return jnp.where(last_lane, 0.0, pltpu.roll(v, width - 1, 1)) - v

    def plus_y(v):
        return jnp.where(last_line, 0.0, pltpu.roll(v, height - 1, 0)) - v

    def minus_z(v):
        return v - jnp.where(first_lane, 0.0, pltpu.roll(v, 1, 1))

    def minus_y(v):
        return v - jnp.where(first_line, 0.0, pltpu.roll(v, 1, 0))

    def sweep(slot, step, runs):
        for run in runs:
            now = [history[slot, run, step, c, 0] for c in range(PARTS)]
            below = None
            for layer in range(layers):
                ex, ey, ez = now
                if layer + 1 < layers:
                    above = [history[slot, run, step, c, layer + 1] for c in range(PARTS)]
                    dx_y, dx_z = above[1] - ey, above[2] - ez
                else:
                    above = None
                    dx_y, dx_z = -ey, -ez
                gx = magnetic[run, 0, layer] - 0.25 * (plus_y(ez) - plus_z(ey))
                gy = magnetic[run, 1, layer] - 0.25 * (plus_z(ex) - dx_z)
                gz = magnetic[run, 2, layer] - 0.25 * (dx_y - plus_y(ex))
                magnetic[run, 0, layer] = gx
                magnetic[run, 1, layer] = gy
                magnetic[run, 2, layer] = gz
                if below is None:
                    bx_y, bx_z = gy, gz
                else:
                    bx_y, bx_z = gy - below[0], gz - below[1]
                below = (gy, gz)
                history[slot, run, step + 1, 0, layer] = keep[0, layer] * ex + (
                    minus_y(gz) - minus_z(gy)
                )
                history[slot, run, step + 1, 1, layer] = keep[1, layer] * ey + (
                    minus_z(gx) - bx_z
                )
                history[slot, run, step + 1, 2, layer] = keep[2, layer] * ez + (
                    bx_y - minus_y(gx)
                )
                now = above

    def one_mesh(mesh, carry):
        slot = lax.rem(mesh, slots)
        for layer in range(layers):
            near = mesh * entries + layer
            for c in range(PARTS):
                lines = pl.ds(c * height, height)
                keep[c, layer] = 1.0 - 0.5 * (picked[near, lines] + picked[near + layers, lines])
        magnetic[...] = jnp.zeros_like(magnetic)
        for copy in incoming(mesh, slot):
            copy.wait()

        @pl.when(mesh >= slots)
        def _():
            outgoing(mesh - slots, slot).wait()

        def step_of(step, inner):
            sweep(slot, step, (0, 1))
            return inner

        lax.fori_loop(0, STEPS - 1, step_of, 0)
        sweep(slot, STEPS - 1, (0,))
        outgoing(mesh, slot).start()
        for layer in range(layers):
            for c in range(PARTS):
                total = None
                for step in range(STEPS):
                    term = (
                        history[slot, 0, step, c, layer]
                        * history[slot, 1, STEPS - 1 - step, c, layer]
                    )
                    total = term if total is None else total + term
                sums[mesh * layers + layer, c * height : (c + 1) * height] = -0.5 * total

        @pl.when(mesh + slots < meshes)
        def _():
            for copy in incoming(mesh + slots, slot):
                copy.start()

        return carry

    lax.fori_loop(0, meshes, one_mesh, 0)

    for which, group in enumerate(back_groups):
        for place, column in enumerate(group):
            for core in range(2):
                for side in range(PLANE):
                    _, mesh, _, layer, share = place_of(column, side, core)
                    values = share * sums[mesh * layers + layer]
                    if side == 0:
                        own_out[2 * column + core] = values
                    else:
                        side_out[which * sides + side - 1][2 * place + core] = values
    for mesh in range(meshes - slots, meshes):
        outgoing(mesh, mesh % slots).wait()


def local(conductivity, block_ids, weights, source, cotangent):
    blocks_here, _, cells = conductivity.shape
    meshes, _, layers, height, width = source.shape
    count = lax.axis_size("dev")
    rows = PARTS * cells // width
    columns = count // (2 * PLANE)
    back_groups = stages(columns)
    sides = range(1, PLANE)
    f32 = jnp.float32
    slow = pl.CostEstimate(flops=0, transcendentals=0, bytes_accessed=1 << 25)

    def swap(value, bits):
        return lax.ppermute(value, "dev", [(i, i ^ bits) for i in range(count)])

    def shape(*dims):
        return jax.ShapeDtypeStruct(dims, f32)

    own = conductivity.reshape(blocks_here, rows, width).transpose(1, 0, 2).reshape(-1, width)
    units = {(column, 0): swap(own, offset(column, 0, 0)) for column in range(columns - 1, 0, -1)}
    units[0, 0] = own
    near = {(side, 0): swap(own, offset(0, side, 0)) for side in sides}
    peer_ids = [swap(block_ids, offset(0, side, 0)) for side in sides]
    for column in range(columns):
        units[column, 1] = swap(units[column, 0], 1)
    for side in sides:
        near[side, 1] = swap(near[side, 0], 1)
    table = pl.pallas_call(
        functools.partial(lookup_kernel, columns, blocks_here),
        out_shape=jax.ShapeDtypeStruct((PLANE, 2 * columns), jnp.int32),
        in_specs=[SMEM] * PLANE,
        out_specs=SMEM,
        scratch_shapes=[pltpu.SMEM((PLANE, count), jnp.int32)],
        compiler_params=limit(16),
        cost_estimate=slow,
        name="lookup",
    )(block_ids, *peer_ids)
    side_in = []
    far = tuple(range(1, columns))
    if far:
        picked = pl.pallas_call(
            functools.partial(gather_kernel, far, blocks_here),
            out_shape=[shape(2 * len(far), rows, width)] * len(sides),
            in_specs=[SMEM] + [VMEM] * (2 * len(far)),
            out_specs=[VMEM] * len(sides),
            compiler_params=limit(16),
            cost_estimate=slow,
            name="collect",
        )(table, *(units[column, core] for column in far for core in range(2)))
        side_in = [swap(value, offset(0, side, 0)) for side, value in zip(sides, picked)]

    slots = min(meshes, 2)
    fields, own_rows, *side_rows = pl.pallas_call(
        functools.partial(mesh_kernel, columns, back_groups, blocks_here),
        out_shape=[shape(*source.shape), shape(2 * columns, rows, width)]
        + [shape(2 * len(group), rows, width) for group in back_groups for _ in sides],
        in_specs=[SMEM, SMEM, HBM, HBM] + [VMEM] * (2 * columns + len(near) + len(side_in)),
        out_specs=[HBM] + [VMEM] * (1 + len(back_groups) * len(sides)),
        scratch_shapes=[
            pltpu.VMEM((slots, 2, STEPS + 1, PARTS, layers, height, width), f32),
            pltpu.VMEM((2, PARTS, layers, height, width), f32),
            pltpu.VMEM((PARTS, layers, height, width), f32),
            pltpu.VMEM((count, rows, width), f32),
            pltpu.VMEM((meshes * layers, rows, width), f32),
            pltpu.SMEM((count,), jnp.int32),
            pltpu.SemaphoreType.DMA((slots, 2)),
            pltpu.SemaphoreType.DMA((slots,)),
        ],
        compiler_params=limit(40),
        name="leapfrog",
    )(
        block_ids,
        weights,
        source,
        cotangent,
        *(units[column, core] for column in range(columns) for core in range(2)),
        *(near[side, core] for side in sides for core in range(2)),
        *side_in,
    )

    returned = {}
    for which, group in enumerate(back_groups):
        pieces = side_rows[which * len(sides) : (which + 1) * len(sides)]
        arrived = [swap(value, offset(0, side, 0)) for side, value in zip(sides, pieces)]
        operands = (table, own_rows, *arrived)
        specs = [SMEM] + [VMEM] * (1 + len(sides))
        partner = pl.pallas_call(
            functools.partial(partner_kernel, group, 1),
            out_shape=shape(len(group), blocks_here, rows, width),
            in_specs=specs,
            out_specs=VMEM,
            compiler_params=limit(16),
            name="partner",
        )(*operands)
        partner = swap(partner, 1)
        totals = pl.pallas_call(
            functools.partial(partner_kernel, group, 0),
            out_shape=[shape(blocks_here, rows, width)] * len(group),
            in_specs=specs + [VMEM],
            out_specs=[VMEM] * len(group),
            compiler_params=limit(16),
            name="column",
        )(*operands, partner)
        for column, total in zip(group, totals):
            returned[column] = swap(total, offset(column, 0, 0)) if column else total
    gradient = pl.pallas_call(
        final_kernel,
        out_shape=shape(rows * blocks_here, width),
        in_specs=[VMEM] * columns,
        out_specs=VMEM,
        compiler_params=limit(16),
        name="total",
    )(*(returned[column] for column in range(columns)))
    gradient = gradient.reshape(rows, blocks_here, width).transpose(1, 0, 2)
    return fields, gradient.reshape(conductivity.shape)


def stages(columns):
    return [group for group in (tuple(range(1, columns)), (0,)) if group]


def solution(mesh):
    placed = (
        P("dev", None, None),
        P("dev", None),
        P("dev", None),
        P("dev", None, None, None, None),
        P("dev", None, None, None, None),
    )

    return jax.shard_map(
        local,
        mesh=mesh,
        in_specs=placed,
        out_specs=(P("dev", None, None, None, None), P("dev", None, None)),
        check_vma=False,
    )
```

time: 75.2 us -> 80.6 us (1.072)
  blocking collectives: 60.8 us -> 0 us
  starting transfers between devices: 0 us -> 33.1 us
  waiting for transfers between devices: 0 us -> 31.7 us
  Pallas kernels: 12.5 us -> 13.8 us
    all_to_all x3 -> x0, blocking collectives: 60.8 us -> none  [the longest x1 23.9 us: local(): lax.all_to_all(grads, 'dev', split_axis=0, concat_axis=0, tiled=True)]
    ppermute x0 -> x30, starting transfers between devices: none -> 33.1 us  [swap(): return lax.ppermute(value, 'dev', [(i, i ^ bits) for i in range(count)])]
    ppermute x0 -> x30, waiting for transfers between devices: none -> 31.7 us  [swap(): return lax.ppermute(value, 'dev', [(i, i ^ bits) for i in range(count)])]
    pallas_call x4 -> x8, Pallas kernels: 12.5 us -> 13.8 us  [the longest x1 8.48 us: local(): pl.pallas_call(functools.partial(mesh_kernel, columns, back_groups, block...]
  transfers between devices with their start and end apart: 0 -> 30, of which waited for: 0 -> 16; matrix products, arithmetic and copies ran while one was open for 0% -> 0% of each run, Pallas kernels for 0% -> 5%
where the time goes in v2:
time: 80.6 us; the launch traced here: 80.5 us
  starting transfers between devices  33.1 us (41%)
  waiting for transfers between devices  31.7 us (39%)
  Pallas kernels  13.8 us (17%)
  local copies, waits for them, and re-layouts  1.01 us (1%)
    ppermute x30, starting transfers between devices, swap(): return lax.ppermute(value, 'dev', [(i, i ^ bits) for i in range(count)])  33.1 us
    ppermute x30, waiting for transfers between devices, swap(): return lax.ppermute(value, 'dev', [(i, i ^ bits) for i in range(count)])  31.7 us
    pallas_call x1, Pallas kernels, local(): pl.pallas_call(functools.partial(mesh_kernel, columns, back_groups, block...  8.48 us
    pallas_call x1, Pallas kernels, local(): pl.pallas_call(functools.partial(lookup_kernel, columns, blocks_here), ou...  1.62 us
  transfers between devices with their start and end apart: 30, of which 16 were waited for; matrix products, arithmetic and copies ran while one was open for 0% of the time, Pallas kernels for 5%

profile of v2, /device:TPU:0, one launch (start us, length us, event | category | flops | bytes accessed | tf_op | source)
XLA Modules:
  0.0 80.5 jit_solution(2433908924670139414)
XLA Ops:
  0.6 5.1 %collective-permute-start.5 = (f32[192,128]{1,0:T(8,128)}, f32[192,128]{1,0:T(8,128)S(1)}, u32[]{:S(2)}, u32[]{:S(2)}) collective-permute-start(f32[192,128]{1,0:T(8,128)} %bitcast.10), channel_id=1, source_target_pairs={{0,24},{1,25},{2,26},{3,27},{4,28},{5,29},{6,30},{7,31},{8,16},{9,... | collective-permute-start | bytes 294920 | tf_op jit(solution)/shard_map/ppermute | solution.py:292
  5.8 0.6 collective-permute-start.1
  6.4 2.6 %collective-permute-start.11 = (f32[192,128]{1,0:T(8,128)}, f32[192,128]{1,0:T(8,128)S(1)}, u32[]{:S(2)}, u32[]{:S(2)}) collective-permute-start(f32[192,128]{1,0:T(8,128)} %bitcast.13), channel_id=1, source_target_pairs={{0,6},{1,7},{2,4},{3,5},{4,2},{5,3},{6,0},{7,1},{8,14},{9,15},{10,... | collective-permute-start | bytes 294920 | tf_op jit(solution)/shard_map/ppermute | solution.py:292
  9.0 0.7 collective-permute-done.5.refs_4_.refs_10_
  9.7 4.6 %collective-permute-done.3.refs_2_.refs_8_ = f32[192,128]{1,0:T(8,128)S(1)} collective-permute-done((f32[192,128]{1,0:T(8,128)}, f32[192,128]{1,0:T(8,128)S(1)}, u32[]{:S(2)}, u32[]{:S(2)}) %collective-permute-start.3) | collective-permute-done | bytes 98336 | tf_op jit(solution)/shard_map/ppermute | solution.py:292
  14.3 2.4 %collective-permute-start.15 = (s32[2,16]{1,0:T(2,128)S(1)}, s32[2,16]{1,0:T(2,128)S(1)}, u32[]{:S(2)}, u32[]{:S(2)}) collective-permute-start(s32[2,16]{1,0:T(2,128)S(1)} %copy-done.3), channel_id=1, source_target_pairs={{0,6},{1,7},{2,4},{3,5},{4,2},{5,3},{6,0},{7,1},{8,14},{9,15},{10,... | collective-permute-start | bytes 392 | tf_op jit(solution)/shard_map/ppermute | solution.py:292
  16.7 2.0 %collective-permute-done.15.refs_3_ = s32[2,16]{1,0:T(2,128)S(1)} collective-permute-done((s32[2,16]{1,0:T(2,128)S(1)}, s32[2,16]{1,0:T(2,128)S(1)}, u32[]{:S(2)}, u32[]{:S(2)}) %collective-permute-start.15) | collective-permute-done | bytes 160 | tf_op jit(solution)/shard_map/ppermute | solution.py:292
  18.7 1.5 %collective-permute-start.14 = (s32[2,16]{1,0:T(2,128)S(1)}, s32[2,16]{1,0:T(2,128)S(1)}, u32[]{:S(2)}, u32[]{:S(2)}) collective-permute-start(s32[2,16]{1,0:T(2,128)S(1)} %copy-done.3), channel_id=1, source_target_pairs={{0,4},{1,5},{2,6},{3,7},{4,0},{5,1},{6,2},{7,3},{8,12},{9,13},{10,... | collective-permute-start | bytes 392 | tf_op jit(solution)/shard_map/ppermute | solution.py:292
  20.3 2.0 %collective-permute-done.14.refs_2_ = s32[2,16]{1,0:T(2,128)S(1)} collective-permute-done((s32[2,16]{1,0:T(2,128)S(1)}, s32[2,16]{1,0:T(2,128)S(1)}, u32[]{:S(2)}, u32[]{:S(2)}) %collective-permute-start.14) | collective-permute-done | bytes 160 | tf_op jit(solution)/shard_map/ppermute | solution.py:292
  22.3 1.5 %collective-permute-start.13 = (s32[2,16]{1,0:T(2,128)S(1)}, s32[2,16]{1,0:T(2,128)S(1)}, u32[]{:S(2)}, u32[]{:S(2)}) collective-permute-start(s32[2,16]{1,0:T(2,128)S(1)} %copy-done.3), channel_id=1, source_target_pairs={{0,2},{1,3},{2,0},{3,1},{4,6},{5,7},{6,4},{7,5},{8,10},{9,11},{10,... | collective-permute-start | bytes 392 | tf_op jit(solution)/shard_map/ppermute | solution.py:292
  23.8 2.1 %collective-permute-done.13.refs_1_ = s32[2,16]{1,0:T(2,128)S(1)} collective-permute-done((s32[2,16]{1,0:T(2,128)S(1)}, s32[2,16]{1,0:T(2,128)S(1)}, u32[]{:S(2)}, u32[]{:S(2)}) %collective-permute-start.13) | collective-permute-done | bytes 160 | tf_op jit(solution)/shard_map/ppermute | solution.py:292
  25.9 1.5 %collective-permute-start.9 = (f32[192,128]{1,0:T(8,128)}, f32[192,128]{1,0:T(8,128)S(1)}, u32[]{:S(2)}, u32[]{:S(2)}) collective-permute-start(f32[192,128]{1,0:T(8,128)} %bitcast.14), channel_id=1, source_target_pairs={{0,4},{1,5},{2,6},{3,7},{4,0},{5,1},{6,2},{7,3},{8,12},{9,13},{10,... | collective-permute-start | bytes 294920 | tf_op jit(solution)/shard_map/ppermute | solution.py:292
  27.4 1.5 %collective-permute-start.7 = (f32[192,128]{1,0:T(8,128)}, f32[192,128]{1,0:T(8,128)S(1)}, u32[]{:S(2)}, u32[]{:S(2)}) collective-permute-start(f32[192,128]{1,0:T(8,128)} %bitcast.15), channel_id=1, source_target_pairs={{0,2},{1,3},{2,0},{3,1},{4,6},{5,7},{6,4},{7,5},{8,10},{9,11},{10,... | collective-permute-start | bytes 294920 | tf_op jit(solution)/shard_map/ppermute | solution.py:292
  28.9 0.5 collective-permute-start.12
  29.4 1.6 %lookup.1.table_ref = s32[4,8]{1,0:T(4,128)S(1)} custom-call(s32[2,16]{1,0:T(2,128)S(1)} %copy-done.3, s32[2,16]{1,0:T(2,128)S(1)} %collective-permute-done.13.refs_1_, s32[2,16]{1,0:T(2,128)S(1)} %collective-permute-done.14.refs_2_, s32[2,16]{1,0:T(2,128)S(1)} %collective-permute-done.15.refs_3_), custom_call_target="tpu_custom_call" | custom-call | bytes 33554432 | tf_op jit(solution)/shard_map/lookup/pallas_call | solution.py:306
  31.1 0.6 collect.1
  31.7 0.6 collective-permute-start.16
  32.3 0.5 collective-permute-start.17
  32.8 2.4 %collective-permute-start.18 = (f32[6,48,128]{2,1,0:T(8,128)S(1)}, f32[6,48,128]{2,1,0:T(8,128)S(1)}, u32[]{:S(2)}, u32[]{:S(2)}) collective-permute-start(f32[6,48,128]{2,1,0:T(8,128)S(1)} %get-tuple-element.18), channel_id=1, source_target_pairs={{0,6},{1,7},{2,4},{3,5},{4,2},{5,3},{6,0},{7,1},{8,14},{9,15},{10,... | collective-permute-start | bytes 442376 | tf_op jit(solution)/shard_map/ppermute | solution.py:292
  35.3 0.5 collective-permute-start.8
  35.8 0.8 collective-permute-done.10.refs_15_
  36.6 0.2 collective-permute-done.8.refs_13_
  36.7 1.8 %collective-permute-done.16.refs_18_ = f32[6,48,128]{2,1,0:T(8,128)S(1)} collective-permute-done((f32[6,48,128]{2,1,0:T(8,128)S(1)}, f32[6,48,128]{2,1,0:T(8,128)S(1)}, u32[]{:S(2)}, u32[]{:S(2)}) %collective-permute-start.16) | collective-permute-done | bytes 147488 | tf_op jit(solution)/shard_map/ppermute | solution.py:292
  38.5 2.5 %collective-permute-done.17.refs_19_ = f32[6,48,128]{2,1,0:T(8,128)S(1)} collective-permute-done((f32[6,48,128]{2,1,0:T(8,128)S(1)}, f32[6,48,128]{2,1,0:T(8,128)S(1)}, u32[]{:S(2)}, u32[]{:S(2)}) %collective-permute-start.17) | collective-permute-done | bytes 147488 | tf_op jit(solution)/shard_map/ppermute | solution.py:292
  41.1 1.0 %copy-done.1 = f32[2,3,8,16,128]{4,3,2,1,0:T(8,128)S(1)} copy-done((f32[2,3,8,16,128]{4,3,2,1,0:T(8,128)S(1)}, f32[2,3,8,16,128]{4,3,2,1,0:T(8,128)}, u32[]{:S(2)}) %copy-start.1) | copy-done | bytes 393240
  42.0 8.5 %leapfrog.1 = (f32[2,3,8,16,128]{4,3,2,1,0:T(8,128)}, f32[8,48,128]{2,1,0:T(8,128)S(1)}, f32[6,48,128]{2,1,0:T(8,128)S(1)}, f32[6,48,128]{2,1,0:T(8,128)S(1)}, f...) custom-call(s32[2,16]{1,0:T(2,128)S(1)} %copy-done.3, ...), custom_call_target="tpu_custom_call" | custom-call | tf_op jit(solution)/shard_map/leapfrog/pallas_call | solution.py:331
  50.5 1.6 %collective-permute-start.23 = (f32[6,48,128]{2,1,0:T(8,128)S(1)}, f32[6,48,128]{2,1,0:T(8,128)S(1)}, u32[]{:S(2)}, u32[]{:S(2)}) collective-permute-start(f32[6,48,128]{2,1,0:T(8,128)S(1)} %get-tuple-element.24), channel_id=1, source_target_pairs={{0,2},{1,3},{2,0},{3,1},{4,6},{5,7},{6,4},{7,5},{8,10},{9,11},{10,... | collective-permute-start | bytes 442376 | tf_op jit(solution)/shard_map/ppermute | solution.py:292
  52.1 0.5 collective-permute-start.24
  52.6 1.5 %collective-permute-start.25 = (f32[6,48,128]{2,1,0:T(8,128)S(1)}, f32[6,48,128]{2,1,0:T(8,128)S(1)}, u32[]{:S(2)}, u32[]{:S(2)}) collective-permute-start(f32[6,48,128]{2,1,0:T(8,128)S(1)} %get-tuple-element.26), channel_id=1, source_target_pairs={{0,6},{1,7},{2,4},{3,5},{4,2},{5,3},{6,0},{7,1},{8,14},{9,15},{10,... | collective-permute-start | bytes 442376 | tf_op jit(solution)/shard_map/ppermute | solution.py:292
  54.1 2.9 %collective-permute-done.23.refs_0_ = f32[6,48,128]{2,1,0:T(8,128)S(1)} collective-permute-done((f32[6,48,128]{2,1,0:T(8,128)S(1)}, f32[6,48,128]{2,1,0:T(8,128)S(1)}, u32[]{:S(2)}, u32[]{:S(2)}) %collective-permute-start.23) | collective-permute-done | bytes 147488 | tf_op jit(solution)/shard_map/ppermute | solution.py:292
  56.9 2.9 %collective-permute-done.24.refs_1_ = f32[6,48,128]{2,1,0:T(8,128)S(1)} collective-permute-done((f32[6,48,128]{2,1,0:T(8,128)S(1)}, f32[6,48,128]{2,1,0:T(8,128)S(1)}, u32[]{:S(2)}, u32[]{:S(2)}) %collective-permute-start.24) | collective-permute-done | bytes 147488 | tf_op jit(solution)/shard_map/ppermute | solution.py:292
  59.8 0.6 partner.3
  60.5 0.1 collective-permute-start.26
  60.6 1.0 %collective-permute-start.19 = (f32[2,48,128]{2,1,0:T(8,128)S(1)}, f32[2,48,128]{2,1,0:T(8,128)S(1)}, u32[]{:S(2)}, u32[]{:S(2)}) collective-permute-start(f32[2,48,128]{2,1,0:T(8,128)S(1)} %get-tuple-element.21), channel_id=1, source_target_pairs={{0,2},{1,3},{2,0},{3,1},{4,6},{5,7},{6,4},{7,5},{8,10},{9,11},{10,... | collective-permute-start | bytes 147464 | tf_op jit(solution)/shard_map/ppermute | solution.py:292
  61.6 0.9 %collective-permute-start.20 = (f32[2,48,128]{2,1,0:T(8,128)S(1)}, f32[2,48,128]{2,1,0:T(8,128)S(1)}, u32[]{:S(2)}, u32[]{:S(2)}) collective-permute-start(f32[2,48,128]{2,1,0:T(8,128)S(1)} %get-tuple-element.22), channel_id=1, source_target_pairs={{0,4},{1,5},{2,6},{3,7},{4,0},{5,1},{6,2},{7,3},{8,12},{9,13},{10,... | collective-permute-start | bytes 147464 | tf_op jit(solution)/shard_map/ppermute | solution.py:292
  62.5 1.7 %collective-permute-start.21 = (f32[2,48,128]{2,1,0:T(8,128)S(1)}, f32[2,48,128]{2,1,0:T(8,128)S(1)}, u32[]{:S(2)}, u32[]{:S(2)}) collective-permute-start(f32[2,48,128]{2,1,0:T(8,128)S(1)} %get-tuple-element.23), channel_id=1, source_target_pairs={{0,6},{1,7},{2,4},{3,5},{4,2},{5,3},{6,0},{7,1},{8,14},{9,15},{10,... | collective-permute-start | bytes 147464 | tf_op jit(solution)/shard_map/ppermute | solution.py:292
  64.1 0.6 collective-permute-done.19.refs_0_
  64.7 1.0 %collective-permute-done.20.refs_1_ = f32[2,48,128]{2,1,0:T(8,128)S(1)} collective-permute-done((f32[2,48,128]{2,1,0:T(8,128)S(1)}, f32[2,48,128]{2,1,0:T(8,128)S(1)}, u32[]{:S(2)}, u32[]{:S(2)}) %collective-permute-start.20) | collective-permute-done | bytes 49184 | tf_op jit(solution)/shard_map/ppermute | solution.py:292
  65.7 1.8 %collective-permute-done.21.refs_2_ = f32[2,48,128]{2,1,0:T(8,128)S(1)} collective-permute-done((f32[2,48,128]{2,1,0:T(8,128)S(1)}, f32[2,48,128]{2,1,0:T(8,128)S(1)}, u32[]{:S(2)}, u32[]{:S(2)}) %collective-permute-start.21) | collective-permute-done | bytes 49184 | tf_op jit(solution)/shard_map/ppermute | solution.py:292
  67.4 0.6 partner.2
  68.0 0.1 collective-permute-start.22
  68.1 0.6 column.3
  68.8 3.1 %collective-permute-start.28 = (f32[4,48,128]{2,1,0:T(8,128)S(1)}, f32[4,48,128]{2,1,0:T(8,128)S(1)}, u32[]{:S(2)}, u32[]{:S(2)}) collective-permute-start(f32[4,48,128]{2,1,0:T(8,128)S(1)} %get-tuple-element.28), channel_id=1, source_target_pairs={{0,16},{1,17},{2,18},{3,19},{4,20},{5,21},{6,22},{7,23},{8,24},{9,... | collective-permute-start | bytes 294920 | tf_op jit(solution)/shard_map/ppermute | solution.py:292
  71.9 1.3 %collective-permute-start.29 = (f32[4,48,128]{2,1,0:T(8,128)S(1)}, f32[4,48,128]{2,1,0:T(8,128)S(1)}, u32[]{:S(2)}, u32[]{:S(2)}) collective-permute-start(f32[4,48,128]{2,1,0:T(8,128)S(1)} %get-tuple-element.29), channel_id=1, source_target_pairs={{0,24},{1,25},{2,26},{3,27},{4,28},{5,29},{6,30},{7,31},{8,16},{9,... | collective-permute-start | bytes 294920 | tf_op jit(solution)/shard_map/ppermute | solution.py:292
  73.2 0.6 column.2.refs_0_
  73.8 1.9 %collective-permute-done.27.refs_1_ = f32[4,48,128]{2,1,0:T(8,128)S(1)} collective-permute-done((f32[4,48,128]{2,1,0:T(8,128)S(1)}, f32[4,48,128]{2,1,0:T(8,128)S(1)}, u32[]{:S(2)}, u32[]{:S(2)}) %collective-permute-start.27) | collective-permute-done | bytes 98336 | tf_op jit(solution)/shard_map/ppermute | solution.py:292
  75.8 4.0 %collective-permute-done.28.refs_2_ = f32[4,48,128]{2,1,0:T(8,128)S(1)} collective-permute-done((f32[4,48,128]{2,1,0:T(8,128)S(1)}, f32[4,48,128]{2,1,0:T(8,128)S(1)}, u32[]{:S(2)}, u32[]{:S(2)}) %collective-permute-start.28) | collective-permute-done | bytes 98336 | tf_op jit(solution)/shard_map/ppermute | solution.py:292
  79.8 0.7 total.1
  (30 shorter events, 0.1 us)
Async XLA Ops:
  0.6 13.6 %copy-start.3 = (s32[2,16]{1,0:T(2,128)S(1)}, s32[2,16]{1,0:T(2,128)}, u32[]{:S(2)}) copy-start(s32[2,16]{1,0:T(2,128)} %refs_0_.3) | copy-start | bytes 388
  0.6 40.4 %copy-start = (f32[2,3,8,16,128]{4,3,2,1,0:T(8,128)S(1)}, f32[2,3,8,16,128]{4,3,2,1,0:T(8,128)}, u32[]{:S(2)}) copy-start(f32[2,3,8,16,128]{4,3,2,1,0:T(8,128)} %refs_2_.1) | copy-start | bytes 1179652
  0.6 9.1 %collective-permute-start.5 = (f32[192,128]{1,0:T(8,128)}, f32[192,128]{1,0:T(8,128)S(1)}, u32[]{:S(2)}, u32[]{:S(2)}) collective-permute-start(f32[192,128]{1,0:T(8,128)} %bitcast.10), channel_id=1, source_target_pairs={{0,24},{1,25},{2,26},{3,27},{4,28},{5,29},{6,30},{7,31},{8,16},{9,... | collective-permute-start | bytes 294920 | tf_op jit(solution)/shard_map/ppermute | solution.py:292
  5.8 8.5 %collective-permute-start.3 = (f32[192,128]{1,0:T(8,128)}, f32[192,128]{1,0:T(8,128)S(1)}, u32[]{:S(2)}, u32[]{:S(2)}) collective-permute-start(f32[192,128]{1,0:T(8,128)} %bitcast.11), channel_id=1, source_target_pairs={{0,16},{1,17},{2,18},{3,19},{4,20},{5,21},{6,22},{7,23},{8,24},{9,... | collective-permute-start | bytes 294920 | tf_op jit(solution)/shard_map/ppermute | solution.py:292
  5.8 14.5 %collective-permute-start.1 = (f32[192,128]{1,0:T(8,128)}, f32[192,128]{1,0:T(8,128)S(1)}, u32[]{:S(2)}, u32[]{:S(2)}) collective-permute-start(f32[192,128]{1,0:T(8,128)} %bitcast.12), channel_id=1, source_target_pairs={{0,8},{1,9},{2,10},{3,11},{4,12},{5,13},{6,14},{7,15},{8,0},{9,1},... | collective-permute-start | bytes 294920 | tf_op jit(solution)/shard_map/ppermute | solution.py:292
  6.4 21.0 %collective-permute-start.11 = (f32[192,128]{1,0:T(8,128)}, f32[192,128]{1,0:T(8,128)S(1)}, u32[]{:S(2)}, u32[]{:S(2)}) collective-permute-start(f32[192,128]{1,0:T(8,128)} %bitcast.13), channel_id=1, source_target_pairs={{0,6},{1,7},{2,4},{3,5},{4,2},{5,3},{6,0},{7,1},{8,14},{9,15},{10,... | collective-permute-start | bytes 294920 | tf_op jit(solution)/shard_map/ppermute | solution.py:292
  9.7 19.2 %collective-permute-start.6 = (f32[192,128]{1,0:T(8,128)S(1)}, f32[192,128]{1,0:T(8,128)S(1)}, u32[]{:S(2)}, u32[]{:S(2)}) collective-permute-start(f32[192,128]{1,0:T(8,128)S(1)} %collective-permute-done.5.refs_4_.refs_10_), channel_id=1, source_target_pairs={{0,1},{1,0},{2,3},{3,2},{4,5},{5,4},{6,7},{7,6},{8,9},{9,8},{10,11... | collective-permute-start | bytes 294920 | tf_op jit(solution)/shard_map/ppermute | solution.py:292
  14.3 14.7 %collective-permute-start.4 = (f32[192,128]{1,0:T(8,128)S(1)}, f32[192,128]{1,0:T(8,128)S(1)}, u32[]{:S(2)}, u32[]{:S(2)}) collective-permute-start(f32[192,128]{1,0:T(8,128)S(1)} %collective-permute-done.3.refs_2_.refs_8_), channel_id=1, source_target_pairs={{0,1},{1,0},{2,3},{3,2},{4,5},{5,4},{6,7},{7,6},{8,9},{9,8},{10,11... | collective-permute-start | bytes 294920 | tf_op jit(solution)/shard_map/ppermute | solution.py:292
  14.3 4.5 %collective-permute-start.15 = (s32[2,16]{1,0:T(2,128)S(1)}, s32[2,16]{1,0:T(2,128)S(1)}, u32[]{:S(2)}, u32[]{:S(2)}) collective-permute-start(s32[2,16]{1,0:T(2,128)S(1)} %copy-done.3), channel_id=1, source_target_pairs={{0,6},{1,7},{2,4},{3,5},{4,2},{5,3},{6,0},{7,1},{8,14},{9,15},{10,... | collective-permute-start | bytes 392 | tf_op jit(solution)/shard_map/ppermute | solution.py:292
  18.7 3.6 %collective-permute-start.14 = (s32[2,16]{1,0:T(2,128)S(1)}, s32[2,16]{1,0:T(2,128)S(1)}, u32[]{:S(2)}, u32[]{:S(2)}) collective-permute-start(s32[2,16]{1,0:T(2,128)S(1)} %copy-done.3), channel_id=1, source_target_pairs={{0,4},{1,5},{2,6},{3,7},{4,0},{5,1},{6,2},{7,3},{8,12},{9,13},{10,... | collective-permute-start | bytes 392 | tf_op jit(solution)/shard_map/ppermute | solution.py:292
  20.3 10.8 %collective-permute-start.2 = (f32[192,128]{1,0:T(8,128)S(1)}, f32[192,128]{1,0:T(8,128)S(1)}, u32[]{:S(2)}, u32[]{:S(2)}) collective-permute-start(f32[192,128]{1,0:T(8,128)S(1)} %collective-permute-done.1.refs_0_.refs_6_), channel_id=1, source_target_pairs={{0,1},{1,0},{2,3},{3,2},{4,5},{5,4},{6,7},{7,6},{8,9},{9,8},{10,11... | collective-permute-start | bytes 294920 | tf_op jit(solution)/shard_map/ppermute | solution.py:292
  22.3 3.6 %collective-permute-start.13 = (s32[2,16]{1,0:T(2,128)S(1)}, s32[2,16]{1,0:T(2,128)S(1)}, u32[]{:S(2)}, u32[]{:S(2)}) collective-permute-start(s32[2,16]{1,0:T(2,128)S(1)} %copy-done.3), channel_id=1, source_target_pairs={{0,2},{1,3},{2,0},{3,1},{4,6},{5,7},{6,4},{7,5},{8,10},{9,11},{10,... | collective-permute-start | bytes 392 | tf_op jit(solution)/shard_map/ppermute | solution.py:292
  25.9 6.4 %collective-permute-start.9 = (f32[192,128]{1,0:T(8,128)}, f32[192,128]{1,0:T(8,128)S(1)}, u32[]{:S(2)}, u32[]{:S(2)}) collective-permute-start(f32[192,128]{1,0:T(8,128)} %bitcast.14), channel_id=1, source_target_pairs={{0,4},{1,5},{2,6},{3,7},{4,0},{5,1},{6,2},{7,3},{8,12},{9,13},{10,... | collective-permute-start | bytes 294920 | tf_op jit(solution)/shard_map/ppermute | solution.py:292
  27.4 5.4 %collective-permute-start.7 = (f32[192,128]{1,0:T(8,128)}, f32[192,128]{1,0:T(8,128)S(1)}, u32[]{:S(2)}, u32[]{:S(2)}) collective-permute-start(f32[192,128]{1,0:T(8,128)} %bitcast.15), channel_id=1, source_target_pairs={{0,2},{1,3},{2,0},{3,1},{4,6},{5,7},{6,4},{7,5},{8,10},{9,11},{10,... | collective-permute-start | bytes 294920 | tf_op jit(solution)/shard_map/ppermute | solution.py:292
  28.9 6.4 %collective-permute-start = (f32[192,128]{1,0:T(8,128)}, f32[192,128]{1,0:T(8,128)S(1)}, u32[]{:S(2)}, u32[]{:S(2)}) collective-permute-start(f32[192,128]{1,0:T(8,128)} %bitcast.16), channel_id=1, source_target_pairs={{0,1},{1,0},{2,3},{3,2},{4,5},{5,4},{6,7},{7,6},{8,9},{9,8},{10,11... | collective-permute-start | bytes 294920 | tf_op jit(solution)/shard_map/ppermute | solution.py:292
  28.9 6.4 %collective-permute-start.12 = (f32[192,128]{1,0:T(8,128)S(1)}, f32[192,128]{1,0:T(8,128)S(1)}, u32[]{:S(2)}, u32[]{:S(2)}) collective-permute-start(f32[192,128]{1,0:T(8,128)S(1)} %collective-permute-done.11.refs_16_), channel_id=1, source_target_pairs={{0,1},{1,0},{2,3},{3,2},{4,5},{5,4},{6,7},{7,6},{8,9},{9,8},{10,11... | collective-permute-start | bytes 294920 | tf_op jit(solution)/shard_map/ppermute | solution.py:292
  31.1 10.0 %copy-start.2 = (f32[4,3,2048]{2,0,1:T(4,128)S(1)}, f32[4,3,2048]{2,0,1:T(4,128)}, u32[]{:S(2)}) copy-start(f32[4,3,2048]{2,0,1:T(4,128)} %param.5) | copy-start | bytes 294916
  31.7 6.8 %collective-permute-start.16 = (f32[6,48,128]{2,1,0:T(8,128)S(1)}, f32[6,48,128]{2,1,0:T(8,128)S(1)}, u32[]{:S(2)}, u32[]{:S(2)}) collective-permute-start(f32[6,48,128]{2,1,0:T(8,128)S(1)} %get-tuple-element.16), channel_id=1, source_target_pairs={{0,2},{1,3},{2,0},{3,1},{4,6},{5,7},{6,4},{7,5},{8,10},{9,11},{10,... | collective-permute-start | bytes 442376 | tf_op jit(solution)/shard_map/ppermute | solution.py:292
  32.3 8.7 %copy-start.4 = (s32[2,8]{1,0:T(2,128)S(1)}, s32[2,8]{1,0:T(2,128)}, u32[]{:S(2)}) copy-start(s32[2,8]{1,0:T(2,128)} %refs_1_.1) | copy-start | bytes 196
  32.3 8.7 %collective-permute-start.17 = (f32[6,48,128]{2,1,0:T(8,128)S(1)}, f32[6,48,128]{2,1,0:T(8,128)S(1)}, u32[]{:S(2)}, u32[]{:S(2)}) collective-permute-start(f32[6,48,128]{2,1,0:T(8,128)S(1)} %get-tuple-element.17), channel_id=1, source_target_pairs={{0,4},{1,5},{2,6},{3,7},{4,0},{5,1},{6,2},{7,3},{8,12},{9,13},{10,... | collective-permute-start | bytes 442376 | tf_op jit(solution)/shard_map/ppermute | solution.py:292
  32.8 8.2 %collective-permute-start.18 = (f32[6,48,128]{2,1,0:T(8,128)S(1)}, f32[6,48,128]{2,1,0:T(8,128)S(1)}, u32[]{:S(2)}, u32[]{:S(2)}) collective-permute-start(f32[6,48,128]{2,1,0:T(8,128)S(1)} %get-tuple-element.18), channel_id=1, source_target_pairs={{0,6},{1,7},{2,4},{3,5},{4,2},{5,3},{6,0},{7,1},{8,14},{9,15},{10,... | collective-permute-start | bytes 442376 | tf_op jit(solution)/shard_map/ppermute | solution.py:292
  35.3 1.3 %collective-permute-start.10 = (f32[192,128]{1,0:T(8,128)S(1)}, f32[192,128]{1,0:T(8,128)S(1)}, u32[]{:S(2)}, u32[]{:S(2)}) collective-permute-start(f32[192,128]{1,0:T(8,128)S(1)} %collective-permute-done.9.refs_14_), channel_id=1, source_target_pairs={{0,1},{1,0},{2,3},{3,2},{4,5},{5,4},{6,7},{7,6},{8,9},{9,8},{10,11... | collective-permute-start | bytes 294920 | tf_op jit(solution)/shard_map/ppermute | solution.py:292
  35.3 1.5 %collective-permute-start.8 = (f32[192,128]{1,0:T(8,128)S(1)}, f32[192,128]{1,0:T(8,128)S(1)}, u32[]{:S(2)}, u32[]{:S(2)}) collective-permute-start(f32[192,128]{1,0:T(8,128)S(1)} %collective-permute-done.7.refs_12_), channel_id=1, source_target_pairs={{0,1},{1,0},{2,3},{3,2},{4,5},{5,4},{6,7},{7,6},{8,9},{9,8},{10,11... | collective-permute-start | bytes 294920 | tf_op jit(solution)/shard_map/ppermute | solution.py:292
  41.0 1.0 %copy-start.1 = (f32[2,3,8,16,128]{4,3,2,1,0:T(8,128)S(1)}, f32[2,3,8,16,128]{4,3,2,1,0:T(8,128)}, u32[]{:S(2)}) copy-start(f32[2,3,8,16,128]{4,3,2,1,0:T(8,128)} %refs_3_.1) | copy-start | bytes 1179652
  50.5 6.4 %collective-permute-start.23 = (f32[6,48,128]{2,1,0:T(8,128)S(1)}, f32[6,48,128]{2,1,0:T(8,128)S(1)}, u32[]{:S(2)}, u32[]{:S(2)}) collective-permute-start(f32[6,48,128]{2,1,0:T(8,128)S(1)} %get-tuple-element.24), channel_id=1, source_target_pairs={{0,2},{1,3},{2,0},{3,1},{4,6},{5,7},{6,4},{7,5},{8,10},{9,11},{10,... | collective-permute-start | bytes 442376 | tf_op jit(solution)/shard_map/ppermute | solution.py:292
  52.1 7.7 %collective-permute-start.24 = (f32[6,48,128]{2,1,0:T(8,128)S(1)}, f32[6,48,128]{2,1,0:T(8,128)S(1)}, u32[]{:S(2)}, u32[]{:S(2)}) collective-permute-start(f32[6,48,128]{2,1,0:T(8,128)S(1)} %get-tuple-element.25), channel_id=1, source_target_pairs={{0,4},{1,5},{2,6},{3,7},{4,0},{5,1},{6,2},{7,3},{8,12},{9,13},{10,... | collective-permute-start | bytes 442376 | tf_op jit(solution)/shard_map/ppermute | solution.py:292
  52.6 7.2 %collective-permute-start.25 = (f32[6,48,128]{2,1,0:T(8,128)S(1)}, f32[6,48,128]{2,1,0:T(8,128)S(1)}, u32[]{:S(2)}, u32[]{:S(2)}) collective-permute-start(f32[6,48,128]{2,1,0:T(8,128)S(1)} %get-tuple-element.26), channel_id=1, source_target_pairs={{0,6},{1,7},{2,4},{3,5},{4,2},{5,3},{6,0},{7,1},{8,14},{9,15},{10,... | collective-permute-start | bytes 442376 | tf_op jit(solution)/shard_map/ppermute | solution.py:292
  60.5 7.6 %collective-permute-start.26 = (f32[3,4,48,128]{3,2,1,0:T(8,128)S(1)}, f32[3,4,48,128]{3,2,1,0:T(8,128)S(1)}, u32[]{:S(2)}, u32[]{:S(2)}) collective-permute-start(f32[3,4,48,128]{3,2,1,0:T(8,128)S(1)} %partner.3), channel_id=1, source_target_pairs={{0,1},{1,0},{2,3},{3,2},{4,5},{5,4},{6,7},{7,6},{8,9},{9,8},{10,11... | collective-permute-start | bytes 884744 | tf_op jit(solution)/shard_map/ppermute | solution.py:292
  60.6 4.2 %collective-permute-start.19 = (f32[2,48,128]{2,1,0:T(8,128)S(1)}, f32[2,48,128]{2,1,0:T(8,128)S(1)}, u32[]{:S(2)}, u32[]{:S(2)}) collective-permute-start(f32[2,48,128]{2,1,0:T(8,128)S(1)} %get-tuple-element.21), channel_id=1, source_target_pairs={{0,2},{1,3},{2,0},{3,1},{4,6},{5,7},{6,4},{7,5},{8,10},{9,11},{10,... | collective-permute-start | bytes 147464 | tf_op jit(solution)/shard_map/ppermute | solution.py:292
  61.6 4.1 %collective-permute-start.20 = (f32[2,48,128]{2,1,0:T(8,128)S(1)}, f32[2,48,128]{2,1,0:T(8,128)S(1)}, u32[]{:S(2)}, u32[]{:S(2)}) collective-permute-start(f32[2,48,128]{2,1,0:T(8,128)S(1)} %get-tuple-element.22), channel_id=1, source_target_pairs={{0,4},{1,5},{2,6},{3,7},{4,0},{5,1},{6,2},{7,3},{8,12},{9,13},{10,... | collective-permute-start | bytes 147464 | tf_op jit(solution)/shard_map/ppermute | solution.py:292
  62.5 5.0 %collective-permute-start.21 = (f32[2,48,128]{2,1,0:T(8,128)S(1)}, f32[2,48,128]{2,1,0:T(8,128)S(1)}, u32[]{:S(2)}, u32[]{:S(2)}) collective-permute-start(f32[2,48,128]{2,1,0:T(8,128)S(1)} %get-tuple-element.23), channel_id=1, source_target_pairs={{0,6},{1,7},{2,4},{3,5},{4,2},{5,3},{6,0},{7,1},{8,14},{9,15},{10,... | collective-permute-start | bytes 147464 | tf_op jit(solution)/shard_map/ppermute | solution.py:292
  68.0 5.2 %collective-permute-start.22 = (f32[1,4,48,128]{3,2,1,0:T(8,128)S(1)}, f32[1,4,48,128]{3,2,1,0:T(8,128)S(1)}, u32[]{:S(2)}, u32[]{:S(2)}) collective-permute-start(f32[1,4,48,128]{3,2,1,0:T(8,128)S(1)} %partner.2), channel_id=1, source_target_pairs={{0,1},{1,0},{2,3},{3,2},{4,5},{5,4},{6,7},{7,6},{8,9},{9,8},{10,11... | collective-permute-start | bytes 294920 | tf_op jit(solution)/shard_map/ppermute | solution.py:292
  68.8 7.0 %collective-permute-start.27 = (f32[4,48,128]{2,1,0:T(8,128)S(1)}, f32[4,48,128]{2,1,0:T(8,128)S(1)}, u32[]{:S(2)}, u32[]{:S(2)}) collective-permute-start(f32[4,48,128]{2,1,0:T(8,128)S(1)} %get-tuple-element.27), channel_id=1, source_target_pairs={{0,8},{1,9},{2,10},{3,11},{4,12},{5,13},{6,14},{7,15},{8,0},{9,1},... | collective-permute-start | bytes 294920 | tf_op jit(solution)/shard_map/ppermute | solution.py:292
  68.8 11.0 %collective-permute-start.28 = (f32[4,48,128]{2,1,0:T(8,128)S(1)}, f32[4,48,128]{2,1,0:T(8,128)S(1)}, u32[]{:S(2)}, u32[]{:S(2)}) collective-permute-start(f32[4,48,128]{2,1,0:T(8,128)S(1)} %get-tuple-element.28), channel_id=1, source_target_pairs={{0,16},{1,17},{2,18},{3,19},{4,20},{5,21},{6,22},{7,23},{8,24},{9,... | collective-permute-start | bytes 294920 | tf_op jit(solution)/shard_map/ppermute | solution.py:292
  71.9 7.9 %collective-permute-start.29 = (f32[4,48,128]{2,1,0:T(8,128)S(1)}, f32[4,48,128]{2,1,0:T(8,128)S(1)}, u32[]{:S(2)}, u32[]{:S(2)}) collective-permute-start(f32[4,48,128]{2,1,0:T(8,128)S(1)} %get-tuple-element.29), channel_id=1, source_target_pairs={{0,24},{1,25},{2,26},{3,27},{4,28},{5,29},{6,30},{7,31},{8,16},{9,... | collective-permute-start | bytes 294920 | tf_op jit(solution)/shard_map/ppermute | solution.py:292
